TPU v7x, 32 devices: a whole 2x2x4 slice. The times are simulated.
32 devices in a mesh: context: 16 (over z, x, core), tensor: 2 (over y).
Axes of the slice: x: 2, y: 2, z: 4, core: 2. Of those that a mesh axis runs over, the one named last changes fastest.
Arguments:
- head_inputs: bfloat16 [2048, 8192], P('context', 'tensor'), may hold values from -6 to 6
- step_sizes: float32 [128, 2048], P('tensor', 'context'), may hold values from 0.5 to 1.5
- decay_rate: float32 [128], P('tensor'), may hold values from 0.000146484375 to 0.05
- input_map: bfloat16 [2048, 1024], P('context', 'tensor'), may hold values from -0.5 to 0.5
- output_map: bfloat16 [2048, 1024], P('context', 'tensor'), may hold values from -0.5 to 0.5
- document: int32 [2048], P('context'), may hold values from 0 to 2, never falling along the last dimension, each value on 1 to 1024 neighbouring positions
- grad_output: bfloat16 [2048, 8192], P(('context', 'tensor')), may hold values from -6 to 6
Outputs:
- grad_inputs: bfloat16 [2048, 8192], P('context', 'tensor')
- grad_steps: float32 [128, 2048], P('tensor', 'context')
- grad_in_map: float32 [2048, 1024], P('context', 'tensor')
- grad_out_map: float32 [2048, 1024], P('context', 'tensor')
Inputs may be any that keep to these rules, and one draw needn't show every extreme that they name: document numbers never fall along the tokens; each document has 1 to 1024 tokens, one exactly 1024.
All inputs are finite; a program needn't handle non-finite values.
Results may differ from a plain program's by a relative error of at most 0.001.
Values may be sent and summed in bfloat16 or wider, within the bound.
A program may use at most 192 MiB of HBM per device.

v0:
```python
import jax
import jax.numpy as jnp
from jax import lax
from jax.sharding import PartitionSpec as P

H = 128
P_SIZE = 64
N = 128
G = 8
BLOCK = 128
HIGH = lax.Precision.HIGHEST


def padded(cells, sides, width):
    for axis, dim in sides:
        count = lax.axis_size(axis)
        ends = count - 1
        head = lax.slice_in_dim(cells, 0, width, axis=dim)
        tail = lax.slice_in_dim(cells, cells.shape[dim] - width, cells.shape[dim], axis=dim)
        cells = jnp.concatenate(
            [
                lax.ppermute(tail, axis, [(i, (i + 1) % count) for i in range(ends)]),
                cells,
                lax.ppermute(head, axis, [((i + 1) % count, i) for i in range(ends)]),
            ],
            axis=dim,
        )
    return cells


def entering(part, axis, combine, identity, reverse):
    count = lax.axis_size(axis)
    place = lax.axis_index(axis)
    ahead = count - 1 - place if reverse else place
    gathered = jax.tree.map(lambda a: lax.all_gather(a, axis), part)
    state = jax.tree.map(lambda a, e: jnp.zeros_like(a) + jnp.asarray(e, a.dtype), part, identity)

    def one(step, state):
        source = count - 1 - step if reverse else step
        return combine(
            state, jax.tree.map(lambda a: lax.dynamic_index_in_dim(a, source, 0, False), gathered)
        )

    return lax.fori_loop(0, ahead, one, state)


def link_pairs(earlier, later):
    decay_late = later[0]
    spread = decay_late.reshape(decay_late.shape + (1,) * (earlier[1].ndim - decay_late.ndim))
    return (earlier[0] * decay_late, spread * earlier[1] + later[1])


def shards(head_inputs, step_sizes, decay_rate, input_map, output_map, document, grad_output):
    heads_here = decay_rate.shape[0]
    tokens_here = head_inputs.shape[0]
    per_group = H // G
    groups_here = heads_here // per_group
    span = min(BLOCK, tokens_here)
    count = tokens_here // span
    local_grads = lax.all_to_all(grad_output, "tensor", split_axis=1, concat_axis=0, tiled=True)
    shifted_ids = document + 1
    rim = padded(shifted_ids, (("context", 0),), 1)
    prev_id = rim[0] - 1
    next_id = rim[-1] - 1
    ids_blocks = document.reshape(count, span)
    prev_blocks = jnp.concatenate([prev_id[None], ids_blocks[:-1, -1]])
    next_blocks = jnp.concatenate([ids_blocks[1:, 0], next_id[None]])
    positions = jnp.arange(span)
    lower = positions[:, None] >= positions[None, :]
    mask_blocks = (ids_blocks[:, :, None] == ids_blocks[:, None, :]) & lower[None]
    steps_heads = step_sizes.reshape(groups_here, per_group, count, span)
    rates = decay_rate.reshape(groups_here, per_group)
    cumul = jnp.cumsum(-rates[:, :, None, None] * steps_heads, axis=-1)
    step_rows = jnp.transpose(step_sizes).reshape(count, span, groups_here, per_group)
    inputs_f = head_inputs.astype(jnp.float32).reshape(count, span, groups_here, per_group, P_SIZE)
    scaled = inputs_f * step_rows[..., None]
    grads_f = local_grads.astype(jnp.float32).reshape(count, span, groups_here, per_group, P_SIZE)
    in_bf = input_map.reshape(count, span, groups_here, N)
    out_bf = output_map.reshape(count, span, groups_here, N)
    in_f = in_bf.astype(jnp.float32)
    out_f = out_bf.astype(jnp.float32)
    differ = cumul[..., :, None] - cumul[..., None, :]
    weights = jnp.where(
        mask_blocks[None, None], jnp.exp(jnp.where(mask_blocks[None, None], differ, 0.0)), 0.0
    )
    last_sum = cumul[..., -1:]
    in_coef = jnp.exp(cumul) * (ids_blocks == prev_blocks[:, None]).astype(jnp.float32)
    out_coef = jnp.exp(last_sum - cumul) * (ids_blocks == next_blocks[:, None]).astype(jnp.float32)
    end_coef = jnp.exp(last_sum - cumul) * (ids_blocks == ids_blocks[:, -1:]).astype(jnp.float32)
    block_link = (ids_blocks[:, -1] == prev_blocks).astype(jnp.float32)
    block_decay = jnp.exp(last_sum[..., 0]) * block_link
    fresh = jnp.einsum("kjgn,ghkj,kjghp->kghnp", in_f, end_coef, scaled, precision=HIGH)
    message = jnp.einsum("kign,ghki,kighp->kghnp", out_f, in_coef, grads_f, precision=HIGH)
    running = jnp.zeros_like(fresh[0])
    running_decay = jnp.ones_like(block_decay[..., 0])
    index = 0
    inner_states = running
    inner_decays = running_decay
    running = block_decay[..., index, None, None] * running + fresh[index]
    running_decay = block_decay[..., index] * running_decay
    later_states = [None] * count
    later_decays = [None] * count
    behind = jnp.zeros_like(message[0])
    behind_decay = jnp.ones_like(block_decay[..., 0])
    index = 0
    later_states[index] = behind
    later_decays[index] = behind_decay
    behind = block_decay[..., index, None, None] * behind + message[index]
    behind_decay = block_decay[..., index] * behind_decay
    _, incoming = entering(
        (running_decay, running),
        "context",
        link_pairs,
        (jnp.ones_like(running_decay), jnp.zeros_like(running)),
        False,
    )
    _, adjoint = entering(
        (behind_decay, behind),
        "context",
        link_pairs,
        (jnp.ones_like(behind_decay), jnp.zeros_like(behind)),
        True,
    )
    entry_states = jnp.stack([inner_decays[..., None, None] * incoming + inner_states], axis=0)
    exit_adjoints = jnp.stack(
        [later_decays[0][..., None, None] * adjoint + later_states[0]], axis=0
    )
    cross = jnp.einsum("kign,kjgn->gkij", out_bf, in_bf, preferred_element_type=jnp.float32)
    mixing = weights * cross[:, None]
    state_rows = jnp.einsum("kign,kghnp,ghki->kighp", out_f, entry_states, in_coef, precision=HIGH)
    adjoint_rows = jnp.einsum(
        "kjgn,kghnp,ghkj->kjghp", in_f, exit_adjoints, out_coef, precision=HIGH
    )
    carried_c = jnp.einsum("kighp,kghnp,ghki->kign", grads_f, entry_states, in_coef, precision=HIGH)
    carried_b = jnp.einsum(
        "kjghp,kghnp,ghkj->kjgn", scaled, exit_adjoints, out_coef, precision=HIGH
    )
    outputs = jnp.einsum("ghkij,kjghp->kighp", mixing, scaled, precision=HIGH) + state_rows
    update = jnp.einsum("ghkij,kighp->kjghp", mixing, grads_f, precision=HIGH) + adjoint_rows
    slope_rows = jnp.sum(grads_f * outputs, axis=-1) - jnp.sum(scaled * update, axis=-1)
    step_rows_part = jnp.sum(inputs_f * update, axis=-1)
    grad_inputs = (
        (update * step_rows[..., None])
        .reshape(tokens_here, heads_here * P_SIZE)
        .astype(jnp.bfloat16)
    )
    products = jnp.einsum("kighp,kjghp->ghkij", grads_f, scaled, precision=HIGH)
    score_grad = jnp.sum(weights * products, axis=1)
    grad_out_map = (
        jnp.einsum("gkij,kjgn->kign", score_grad, in_f, precision=HIGH) + carried_c
    ).reshape(tokens_here, groups_here * N)
    grad_in_map = (
        jnp.einsum("gkij,kign->kjgn", score_grad, out_f, precision=HIGH) + carried_b
    ).reshape(tokens_here, groups_here * N)
    slopes = jnp.transpose(slope_rows, (2, 3, 0, 1)).reshape(heads_here, tokens_here)
    step_terms = jnp.transpose(step_rows_part, (2, 3, 0, 1)).reshape(heads_here, tokens_here)
    token_index = jnp.arange(tokens_here)
    same_doc = (document[:, None] == document[None, :]) & (
        token_index[:, None] >= token_index[None, :]
    )
    tails_local = jnp.dot(
        slopes, same_doc.astype(jnp.float32), precision=HIGH, preferred_element_type=jnp.float32
    )
    tail_message = jnp.sum(slopes * (document == prev_id).astype(jnp.float32)[None, :], axis=1)
    linked = (document[-1] == prev_id).astype(jnp.float32)
    tail_link = linked * jnp.ones((heads_here,), jnp.float32)
    _, tail_carry = entering(
        (tail_link, tail_message),
        "context",
        link_pairs,
        (jnp.ones_like(tail_link), jnp.zeros_like(tail_message)),
        True,
    )
    tails = tails_local + tail_carry[:, None] * (document == next_id).astype(jnp.float32)[None, :]
    grad_steps = step_terms - decay_rate[:, None] * tails
    return (grad_inputs, grad_steps, grad_in_map, grad_out_map)


def solution(mesh):
    placed = (
        P("context", "tensor"),
        P("tensor", "context"),
        P("tensor"),
        P("context", "tensor"),
        P("context", "tensor"),
        P("context"),
        P(("context", "tensor"), None),
    )
    return jax.shard_map(
        shards,
        mesh=mesh,
        in_specs=placed,
        out_specs=(
            P("context", "tensor"),
            P("tensor", "context"),
            P("context", "tensor"),
            P("context", "tensor"),
        ),
        check_vma=False,
    )
```

profile of v0, /device:TPU:0, one launch (start us, length us, event | category | flops | bytes accessed | tf_op | source)
XLA Modules:
  0.0 581.5 jit_solution(4755453482523883967)
XLA Ops:
  8.5 2.9 collective-permute-start.1
  27.4 3.6 all-to-all-start
  32.0 12.9 %all-to-all-done = bf16[64,2,4096]{2,0,1:T(8,128)(2,1)S(1)} async-done(((bf16[64,2,4096]{2,0,1:T(8,128)(2,1)}), bf16[64,2,4096]{2,0,1:T(8,128)(2,1)S(1)}, u32[]{:S(2)}, u32[]{:S(2)}) %all-to-all-start) | async-done | bytes 1048608 | tf_op jit(solution)/shard_map/all_to_all | solution.py:60
  44.9 3.3 reshape.364
  48.2 4.0 copy.98
  52.2 3.8 fusion.14
  60.3 6.9 %fusion.2 = f32[4,16,64,128]{3,2,1,0:T(8,128)} fusion(f32[4,128,128]{1,2,0:T(8,128)S(1)} %fusion.62, f32[4,16,128]{2,1,0:T(8,128)} %bitcast.206, pred[128,128]{0,1:T(8,128)(4,1)S(1)} %fusion.55, f32[128,4,16,64]{0,3,2,1:T(8,128)S(1)} %bitcast.183, f32[128,4,16]{0,2,1:T(8,128)} %bitcast.198), kind=kOutput, calls=%fused_computation.12 | convolution fusion | flops 810024960 | bytes 4538368 | tf_op jit(solution)/shard_map/ghkij,kjghp->kighp/dot_general | solution.py:138
  70.3 35.9 %all-reduce = f32[16]{0:T(128)} all-reduce(f32[16]{0:T(128)} %dynamic-update-slice), channel_id=2, replica_groups=mesh['context'=16,'tensor'=2] {'context'}, use_global_device_ids=true, to_apply=%add | all-reduce | flops 16 | bytes 128
  106.2 19.4 %all-gather = f32[64,16,1,1]{1,3,2,0:T(1,128)} all-gather(f32[4,16,1,1]{1,3,2,0:T(1,128)} %bitcast.214), channel_id=3, replica_groups=mesh['context'=16,'tensor'=2] {'context'}, dimensions={0}, use_global_device_ids=true | all-gather | bytes 4352 | tf_op jit(solution)/shard_map/all_gather | solution.py:35
  127.2 4.6 reshape.373
  131.8 4.9 copy.112
  136.7 5.7 fusion
  144.5 6.2 %fusion.4 = f32[4,16,128,64]{2,3,1,0:T(8,128)} fusion(bf16[128,4,16,64]{0,3,2,1:T(8,128)(2,1)S(1)} %copy-done.2, f32[4,128,128]{1,2,0:T(8,128)S(1)} %copy-done.13, f32[4,16,128]{2,1,0:T(8,128)S(1)} %bitcast.208, pred[128,128]{0,1:T(8,128)(4,1)S(1)} %fusion.55), kind=kOutput, calls=%fused_computation.13 | convolution fusion | flops 809500672 | bytes 3457024 | tf_op jit(solution)/shard_map/ghkij,kighp->kjghp/dot_general | solution.py:139
  150.7 47.4 %all-gather.7.cloned.1.call-done = f32[16,4,16,128,64]{3,4,2,1,0:T(8,128)} async-done(((f32[1,4,16,128,64]{3,4,2,1,0:T(8,128)}), f32[16,4,16,128,64]{3,4,2,1,0:T(8,128)}) %all-gather.7.cloned.1.call-update) | async-done | bytes 33554448 | tf_op jit(solution)/shard_map/all_gather | solution.py:35
  201.3 6.8 %fusion.38 = f32[1,128,4,128]{1,3,2,0:T(8,128)} fusion(f32[1,128,4,128]{1,3,2,0:T(8,128)} %convolution_bitcast_fusion, f32[4,16,128,64]{3,2,1,0:T(8,128)} %get-tuple-element.217, bf16[128,4,16,64]{0,3,2,1:T(8,128)(2,1)S(1)} %copy-done.2, f32[4,16,128]{2,1,0:T(8,128)S(1)} %copy-done.9), kind=kOutput, calls=%fused_computation.55 | convolution fusion | flops 806420480 | bytes 3702784 | tf_op jit(solution)/shard_map/kighp,kghnp,ghki->kign/dot_general | solution.py:134
  210.0 6.9 %fusion.11 = f32[128,4,16]{0,2,1:T(8,128)} fusion(f32[1,128,4,16,64]{1,4,3,2,0:T(8,128)S(1)} %copy-done.3, f32[4,16,64,128]{3,2,1,0:T(8,128)} %fusion.2, f32[4,16,128,64]{3,2,1,0:T(8,128)} %get-tuple-element.217, f32[128,4,16]{0,2,1:T(8,128)S(1)} %bitcast.204, bf16[128,4,128,1]{2,1,0,3:T(4,128)(2,1)S(1)} %bitcast.193), kind=kOutput, calls=%fused_computation.21 | convolution fusion | flops 807395328 | bytes 6488064 | tf_op jit(solution)/shard_map/kign,kghnp,ghki->kighp/dot_general | solution.py:130
  216.9 151.2 %all-gather.5.cloned.1.call-done = f32[16,4,16,128,64]{3,4,2,1,0:T(8,128)} async-done(((f32[1,4,16,128,64]{3,4,2,1,0:T(8,128)}), f32[16,4,16,128,64]{3,4,2,1,0:T(8,128)}) %all-gather.5.cloned.1.call-update) | async-done | bytes 33554448 | tf_op jit(solution)/shard_map/all_gather | solution.py:35
  370.7 167.5 %while.40 = (s32[]{:T(128)}, f32[4,16,128,64]{3,2,1,0:T(8,128)}, s32[]{:T(128)}, f32[16,4,16]{2,1,0:T(4,128)}, f32[16,4,16,128,64]{3,4,2,1,0:T(8,128)}, /*index=5*/s32[]{:T(128)}, s32[]{:T(128)}, s32[]{:T(128)}, s32[]{:T(128)}) while((s32[]{:T(128)}, f32[4,16,128,64]{3,2,1,0:T(8,128)}, s32[]{:T(128)}, f32[16,4,16]{2,1,0:T(4,128)}, ...), condition=%wide.region_2.3_spmd, body=%wide.region_1.2_spmd.sunk | while | flops 1048582 | bytes 14680979 | solution.py:44
  372.5 2.8 copy.164
  375.9 6.0 %bitcast_add_fusion.10 = f32[4,16,128,64]{3,2,1,0:T(8,128)} fusion(f32[1,4,16,128,64]{4,3,2,1,0:T(8,128)} %copy.164, f32[4,16,128,64]{3,2,1,0:T(8,128)} %get-tuple-element.426, f32[4,16]{1,0:T(4,128)S(1)} %dynamic-slice_bitcast_fusion.4), kind=kLoop, calls=%fused_computation.clone.1 | loop fusion | flops 1048576 | bytes 6291712 | tf_op jit(solution)/shard_map/while/body/add | solution.py:50
  387.0 6.0 %bitcast_add_fusion.10 = f32[4,16,128,64]{3,2,1,0:T(8,128)} fusion(f32[1,4,16,128,64]{4,3,2,1,0:T(8,128)} %copy.164, f32[4,16,128,64]{3,2,1,0:T(8,128)} %get-tuple-element.426, f32[4,16]{1,0:T(4,128)S(1)} %dynamic-slice_bitcast_fusion.4), kind=kLoop, calls=%fused_computation.clone.1 | loop fusion | flops 1048576 | bytes 6291712 | tf_op jit(solution)/shard_map/while/body/add | solution.py:50
  394.8 2.8 copy.164
  398.2 6.0 %bitcast_add_fusion.10 = f32[4,16,128,64]{3,2,1,0:T(8,128)} fusion(f32[1,4,16,128,64]{4,3,2,1,0:T(8,128)} %copy.164, f32[4,16,128,64]{3,2,1,0:T(8,128)} %get-tuple-element.426, f32[4,16]{1,0:T(4,128)S(1)} %dynamic-slice_bitcast_fusion.4), kind=kLoop, calls=%fused_computation.clone.1 | loop fusion | flops 1048576 | bytes 6291712 | tf_op jit(solution)/shard_map/while/body/add | solution.py:50
  405.9 2.8 copy.164
  409.3 6.0 %bitcast_add_fusion.10 = f32[4,16,128,64]{3,2,1,0:T(8,128)} fusion(f32[1,4,16,128,64]{4,3,2,1,0:T(8,128)} %copy.164, f32[4,16,128,64]{3,2,1,0:T(8,128)} %get-tuple-element.426, f32[4,16]{1,0:T(4,128)S(1)} %dynamic-slice_bitcast_fusion.4), kind=kLoop, calls=%fused_computation.clone.1 | loop fusion | flops 1048576 | bytes 6291712 | tf_op jit(solution)/shard_map/while/body/add | solution.py:50
  417.1 2.8 copy.164
  420.5 6.0 %bitcast_add_fusion.10 = f32[4,16,128,64]{3,2,1,0:T(8,128)} fusion(f32[1,4,16,128,64]{4,3,2,1,0:T(8,128)} %copy.164, f32[4,16,128,64]{3,2,1,0:T(8,128)} %get-tuple-element.426, f32[4,16]{1,0:T(4,128)S(1)} %dynamic-slice_bitcast_fusion.4), kind=kLoop, calls=%fused_computation.clone.1 | loop fusion | flops 1048576 | bytes 6291712 | tf_op jit(solution)/shard_map/while/body/add | solution.py:50
  428.3 2.8 copy.164
  431.7 6.0 %bitcast_add_fusion.10 = f32[4,16,128,64]{3,2,1,0:T(8,128)} fusion(f32[1,4,16,128,64]{4,3,2,1,0:T(8,128)} %copy.164, f32[4,16,128,64]{3,2,1,0:T(8,128)} %get-tuple-element.426, f32[4,16]{1,0:T(4,128)S(1)} %dynamic-slice_bitcast_fusion.4), kind=kLoop, calls=%fused_computation.clone.1 | loop fusion | flops 1048576 | bytes 6291712 | tf_op jit(solution)/shard_map/while/body/add | solution.py:50
  439.4 2.8 copy.164
  442.9 6.0 %bitcast_add_fusion.10 = f32[4,16,128,64]{3,2,1,0:T(8,128)} fusion(f32[1,4,16,128,64]{4,3,2,1,0:T(8,128)} %copy.164, f32[4,16,128,64]{3,2,1,0:T(8,128)} %get-tuple-element.426, f32[4,16]{1,0:T(4,128)S(1)} %dynamic-slice_bitcast_fusion.4), kind=kLoop, calls=%fused_computation.clone.1 | loop fusion | flops 1048576 | bytes 6291712 | tf_op jit(solution)/shard_map/while/body/add | solution.py:50
  450.6 2.8 copy.164
  454.0 6.0 %bitcast_add_fusion.10 = f32[4,16,128,64]{3,2,1,0:T(8,128)} fusion(f32[1,4,16,128,64]{4,3,2,1,0:T(8,128)} %copy.164, f32[4,16,128,64]{3,2,1,0:T(8,128)} %get-tuple-element.426, f32[4,16]{1,0:T(4,128)S(1)} %dynamic-slice_bitcast_fusion.4), kind=kLoop, calls=%fused_computation.clone.1 | loop fusion | flops 1048576 | bytes 6291712 | tf_op jit(solution)/shard_map/while/body/add | solution.py:50
  461.8 2.8 copy.164
  465.2 6.0 %bitcast_add_fusion.10 = f32[4,16,128,64]{3,2,1,0:T(8,128)} fusion(f32[1,4,16,128,64]{4,3,2,1,0:T(8,128)} %copy.164, f32[4,16,128,64]{3,2,1,0:T(8,128)} %get-tuple-element.426, f32[4,16]{1,0:T(4,128)S(1)} %dynamic-slice_bitcast_fusion.4), kind=kLoop, calls=%fused_computation.clone.1 | loop fusion | flops 1048576 | bytes 6291712 | tf_op jit(solution)/shard_map/while/body/add | solution.py:50
  472.9 2.8 copy.164
  476.4 6.0 %bitcast_add_fusion.10 = f32[4,16,128,64]{3,2,1,0:T(8,128)} fusion(f32[1,4,16,128,64]{4,3,2,1,0:T(8,128)} %copy.164, f32[4,16,128,64]{3,2,1,0:T(8,128)} %get-tuple-element.426, f32[4,16]{1,0:T(4,128)S(1)} %dynamic-slice_bitcast_fusion.4), kind=kLoop, calls=%fused_computation.clone.1 | loop fusion | flops 1048576 | bytes 6291712 | tf_op jit(solution)/shard_map/while/body/add | solution.py:50
  484.1 2.8 copy.164
  487.5 6.0 %bitcast_add_fusion.10 = f32[4,16,128,64]{3,2,1,0:T(8,128)} fusion(f32[1,4,16,128,64]{4,3,2,1,0:T(8,128)} %copy.164, f32[4,16,128,64]{3,2,1,0:T(8,128)} %get-tuple-element.426, f32[4,16]{1,0:T(4,128)S(1)} %dynamic-slice_bitcast_fusion.4), kind=kLoop, calls=%fused_computation.clone.1 | loop fusion | flops 1048576 | bytes 6291712 | tf_op jit(solution)/shard_map/while/body/add | solution.py:50
  495.3 2.8 copy.164
  498.7 6.0 %bitcast_add_fusion.10 = f32[4,16,128,64]{3,2,1,0:T(8,128)} fusion(f32[1,4,16,128,64]{4,3,2,1,0:T(8,128)} %copy.164, f32[4,16,128,64]{3,2,1,0:T(8,128)} %get-tuple-element.426, f32[4,16]{1,0:T(4,128)S(1)} %dynamic-slice_bitcast_fusion.4), kind=kLoop, calls=%fused_computation.clone.1 | loop fusion | flops 1048576 | bytes 6291712 | tf_op jit(solution)/shard_map/while/body/add | solution.py:50
  506.4 2.8 copy.164
  509.9 6.0 %bitcast_add_fusion.10 = f32[4,16,128,64]{3,2,1,0:T(8,128)} fusion(f32[1,4,16,128,64]{4,3,2,1,0:T(8,128)} %copy.164, f32[4,16,128,64]{3,2,1,0:T(8,128)} %get-tuple-element.426, f32[4,16]{1,0:T(4,128)S(1)} %dynamic-slice_bitcast_fusion.4), kind=kLoop, calls=%fused_computation.clone.1 | loop fusion | flops 1048576 | bytes 6291712 | tf_op jit(solution)/shard_map/while/body/add | solution.py:50
  521.0 6.0 %bitcast_add_fusion.10 = f32[4,16,128,64]{3,2,1,0:T(8,128)} fusion(f32[1,4,16,128,64]{4,3,2,1,0:T(8,128)} %copy.164, f32[4,16,128,64]{3,2,1,0:T(8,128)} %get-tuple-element.426, f32[4,16]{1,0:T(4,128)S(1)} %dynamic-slice_bitcast_fusion.4), kind=kLoop, calls=%fused_computation.clone.1 | loop fusion | flops 1048576 | bytes 6291712 | tf_op jit(solution)/shard_map/while/body/add | solution.py:50
  532.2 6.0 %bitcast_add_fusion.10 = f32[4,16,128,64]{3,2,1,0:T(8,128)} fusion(f32[1,4,16,128,64]{4,3,2,1,0:T(8,128)} %copy.164, f32[4,16,128,64]{3,2,1,0:T(8,128)} %get-tuple-element.426, f32[4,16]{1,0:T(4,128)S(1)} %dynamic-slice_bitcast_fusion.4), kind=kLoop, calls=%fused_computation.clone.1 | loop fusion | flops 1048576 | bytes 6291712 | tf_op jit(solution)/shard_map/while/body/add | solution.py:50
  538.3 7.7 %multiply_reduce_fusion = (f32[128,4,16]{0,2,1:T(8,128)S(1)}, f32[128,4,16]{0,2,1:T(8,128)}, bf16[1,128,4,16,64]{1,4,3,2,0:T(8,128)(2,1)S(1)}) fusion(f32[1,128,4,16,64]{1,4,3,2,0:T(8,128)} %bitcast.185, f32[128,4,16]{0,2,1:T(8,128)} %bitcast.200, f32[4,16,128,64]{3,2,1,0:T(8,128)} %get-tuple-element.216, bf16[128,4,128,1]{2,1,0,3:T(4,128)(2,1)S(1)} %bitcast.191, ...), kind=kOutput, calls=%fused_computation.31 | convolution fusion | flops 810008576 | bytes 7602176 | tf_op jit(solution)/shard_map/kjgn,kghnp,ghkj->kjghp/dot_general | solution.py:131
  546.1 17.0 %all-gather.1 = f32[16,1,64]{2,1,0:T(1,128)S(1)} all-gather(f32[1,1,64]{2,1,0:T(1,128)S(1)} %reshape.380), channel_id=1, replica_groups=mesh['context'=16,'tensor'=2] {'context'}, dimensions={0}, use_global_device_ids=true | all-gather | bytes 4352 | tf_op jit(solution)/shard_map/all_gather | solution.py:35
  563.9 6.7 %fusion.34 = f32[1,128,4,128]{1,3,2,0:T(8,128)} fusion(f32[1,128,4,128]{1,3,2,0:T(8,128)S(1)} %copy-done.6, f32[4,16,128,64]{3,2,1,0:T(8,128)} %get-tuple-element.216, f32[128,4,16,64]{0,3,2,1:T(8,128)S(1)} %bitcast.186, f32[4,16,128]{2,1,0:T(8,128)} %get-tuple-element.313, f32[128,4,16]{0,2,1:T(8,128)} %bitcast.201), kind=kOutput, calls=%fused_computation.53 | convolution fusion | flops 806420480 | bytes 4784128 | tf_op jit(solution)/shard_map/kjghp,kghnp,ghkj->kjgn/dot_general | solution.py:135
  (148 shorter events, 83.7 us)
Async XLA Ops:
  7.2 190.9 %all-gather.7.cloned.1.call-start = ((), (), s32[]{:S(2)}) async-start(), calls=%async_computation.2 | async-start | bytes 35651584 | tf_op jit(solution)/shard_map/all_gather | solution.py:35
  8.5 10.2 %collective-permute-start.1 = (s32[1]{0:T(128)}, s32[1]{0:T(128)}, u32[]{:S(2)}, u32[]{:S(2)}) collective-permute-start(s32[1]{0:T(128)} %get-tuple-element.319), channel_id=1, source_target_pairs={{0,2},{2,4},{4,6},{6,8},{8,10},{10,12},{12,14},{14,16},{16,18},{18... | collective-permute-start | bytes 20 | tf_op jit(solution)/shard_map/ppermute | solution.py:22
  11.4 9.2 %collective-permute-start = (s32[1]{0:T(128)}, s32[1]{0:T(128)}, u32[]{:S(2)}, u32[]{:S(2)}) collective-permute-start(s32[1]{0:T(128)} %get-tuple-element.318), channel_id=1, source_target_pairs={{2,0},{4,2},{6,4},{8,6},{10,8},{12,10},{14,12},{16,14},{18,16},{20... | collective-permute-start | bytes 20 | tf_op jit(solution)/shard_map/ppermute | solution.py:24
  16.6 5.3 copy-start.10
  16.8 1.8 copy-start.15
  18.5 2.8 copy-start.19
  18.5 4.1 copy-start.7
  18.6 118.0 %copy-start = (f32[128,4096]{0,1:T(8,128)}, f32[128,4096]{0,1:T(8,128)S(1)}, u32[]{:S(2)}) copy-start(f32[128,4096]{0,1:T(8,128)S(1)} %convert_element_type.47) | copy-start | bytes 6291460
  21.9 3.3 copy-start.17
  21.9 3.3 copy-start.21
  22.6 29.6 %copy-start.8 = (f32[4,16,128]{2,1,0:T(8,128)}, f32[4,16,128]{2,1,0:T(8,128)S(1)}, u32[]{:S(2)}) copy-start(f32[4,16,128]{2,1,0:T(8,128)S(1)} %get-tuple-element.314) | copy-start | bytes 98308
  25.2 1.2 copy-start.5
  27.4 17.5 %all-to-all-start = ((bf16[64,2,4096]{2,0,1:T(8,128)(2,1)}), bf16[64,2,4096]{2,0,1:T(8,128)(2,1)S(1)}, u32[]{:S(2)}, u32[]{:S(2)}) async-start(bf16[64,2,4096]{2,0,1:T(8,128)(2,1)} %bitcast.189), calls=%async_computation | async-start | bytes 2097152 | tf_op jit(solution)/shard_map/all_to_all | solution.py:60
  31.1 337.1 %all-gather.5.cloned.1.call-start = ((), (), s32[]{:S(2)}) async-start(), calls=%async_computation.1 | async-start | bytes 35651584 | tf_op jit(solution)/shard_map/all_gather | solution.py:35
  56.0 1.6 copy-start.25
  60.2 6.9 %copy-start.12 = (f32[4,128,128]{1,2,0:T(8,128)}, f32[4,128,128]{1,2,0:T(8,128)S(1)}, u32[]{:S(2)}) copy-start(f32[4,128,128]{1,2,0:T(8,128)S(1)} %fusion.62) | copy-start | bytes 786436
  131.8 4.9 copy-start.2
  136.7 5.7 copy-start.4
  136.7 7.8 %copy-start.11 = (f32[4,16,1,128]{3,1,2,0:T(8,128)S(1)}, f32[4,16,1,128]{3,1,2,0:T(8,128)}, u32[]{:S(2)}) copy-start(f32[4,16,1,128]{3,1,2,0:T(8,128)} %copy-done.10) | copy-start | bytes 98308
  136.7 7.8 %copy-start.13 = (f32[4,128,128]{1,2,0:T(8,128)S(1)}, f32[4,128,128]{1,2,0:T(8,128)}, u32[]{:S(2)}) copy-start(f32[4,128,128]{1,2,0:T(8,128)} %copy-done.12) | copy-start | bytes 786436
  200.6 0.8 copy-start.9
  201.3 8.6 %copy-start.3 = (f32[1,128,4,16,64]{1,4,3,2,0:T(8,128)S(1)}, f32[1,128,4,16,64]{1,4,3,2,0:T(8,128)}, u32[]{:S(2)}) copy-start(f32[1,128,4,16,64]{1,4,3,2,0:T(8,128)} %copy.112) | copy-start | bytes 6291460
  538.2 7.7 %copy-start.14 = (f32[128,4,16]{0,2,1:T(8,128)S(1)}, f32[128,4,16]{0,2,1:T(8,128)}, u32[]{:S(2)}) copy-start(f32[128,4,16]{0,2,1:T(8,128)} %fusion.11) | copy-start | bytes 98308
  538.2 7.7 %copy-start.18 = (f32[128]{0:T(128)S(1)}, f32[128]{0:T(128)}, u32[]{:S(2)}) copy-start(f32[128]{0:T(128)} %copy-done.17) | copy-start | bytes 1540
  538.2 24.9 %copy-start.23 = (f32[16]{0:T(128)S(1)}, f32[16]{0:T(128)}, u32[]{:S(2)}) copy-start(f32[16]{0:T(128)} %all-reduce) | copy-start | bytes 196
  538.2 25.6 %copy-start.1 = (f32[128,4096]{0,1:T(8,128)S(1)}, f32[128,4096]{0,1:T(8,128)}, u32[]{:S(2)}) copy-start(f32[128,4096]{0,1:T(8,128)} %copy-done) | copy-start | bytes 6291460
  538.2 25.6 %copy-start.6 = (f32[1,128,4,128]{1,3,2,0:T(8,128)S(1)}, f32[1,128,4,128]{1,3,2,0:T(8,128)}, u32[]{:S(2)}) copy-start(f32[1,128,4,128]{1,3,2,0:T(8,128)} %convolution_bitcast_fusion.1) | copy-start | bytes 786436
  570.6 3.1 copy-start.16
  570.6 3.1 copy-start.20
  570.6 3.1 copy-start.22
  570.6 3.1 copy-start.24
Sparse Core Ops, SparseCore 0:
  25.3 172.7 all-gather.6
  199.7 168.4 all-gather.4
where the time goes:
time: 583 us; the launch traced here: 581 us
  waiting for transfers between devices  212 us (36%)
  local copies, waits for them, and re-layouts  117 us (20%)
  other arithmetic  98.1 us (17%)
  blocking collectives  72.3 us (12%)
  matrix products  57.4 us (10%)
  between operations  16.9 us (3%)
  starting transfers between devices  7.87 us (1%)
    all_gather x2, waiting for transfers between devices, entering(): gathered = jax.tree.map(lambda a: lax.all_gather(a, axis), part)  199 us
    add x30, other arithmetic, link_pairs(): return (earlier[0] * decay_late, spread * earlier[1] + later[1])  90.3 us
    dynamic_slice x30, local copies, waits for them, and re-layouts, one(): lax.dynamic_index_in_dim(a, source, 0, False)  67.3 us
    all_gather x2, blocking collectives, entering(): gathered = jax.tree.map(lambda a: lax.all_gather(a, axis), part)  36.4 us
    unnamed x1, blocking collectives  35.9 us
    another operation x8, local copies, waits for them, and re-layouts  14.3 us
    all_to_all x1, waiting for transfers between devices, shards(): lax.all_to_all(grad_output, 'tensor', split_axis=1, concat_axis=0, tiled=...  12.9 us
    unnamed x62, local copies, waits for them, and re-layouts  12.1 us
  transfers between devices with their start and end apart: 5, of which 3 were waited for; matrix products, arithmetic and copies ran while one was open for 13% of the time, Pallas kernels for 0%

commit v1 on v0

--- a/solution.py
+++ b/solution.py
@@ -57,7 +57,16 @@
     groups_here = heads_here // per_group
     span = min(BLOCK, tokens_here)
     count = tokens_here // span
-    local_grads = lax.all_to_all(grad_output, "tensor", split_axis=1, concat_axis=0, tiled=True)
+    pack_rings = lambda t0: jnp.concatenate(
+        jax.lax.all_to_all(
+            jnp.stack(jnp.split(t0, jax.lax.axis_size("tensor"), 1)),
+            axis_name="tensor",
+            split_axis=0,
+            concat_axis=0,
+        ),
+        axis=0,
+    )
+    local_grads = pack_rings(grad_output)
     shifted_ids = document + 1
     rim = padded(shifted_ids, (("context", 0),), 1)
     prev_id = rim[0] - 1

time: 583 us -> 584 us (level)
    another operation x8 -> x9, local copies, waits for them, and re-layouts: 14.3 us -> 16.5 us
    unnamed x62 -> x58, local copies, waits for them, and re-layouts: 12.1 us -> 10.8 us
where the time goes in v1:
time: 584 us; the launch traced here: 582 us
  waiting for transfers between devices  214 us (37%)
  local copies, waits for them, and re-layouts  115 us (20%)
  other arithmetic  97.7 us (17%)
  blocking collectives  72.4 us (12%)
  matrix products  57.8 us (10%)
  between operations  16.9 us (3%)
  starting transfers between devices  7.99 us (1%)
    all_gather x2, waiting for transfers between devices, entering(): gathered = jax.tree.map(lambda a: lax.all_gather(a, axis), part)  201 us
    add x30, other arithmetic, link_pairs(): return (earlier[0] * decay_late, spread * earlier[1] + later[1])  90.4 us
    dynamic_slice x30, local copies, waits for them, and re-layouts, one(): lax.dynamic_index_in_dim(a, source, 0, False)  67.4 us
    all_gather x2, blocking collectives, entering(): gathered = jax.tree.map(lambda a: lax.all_gather(a, axis), part)  36.5 us
    unnamed x1, blocking collectives  36 us
    another operation x8, local copies, waits for them, and re-layouts  15.2 us
    all_to_all x1, waiting for transfers between devices, shards(): jax.lax.all_to_all(jnp.stack(jnp.split(t0, jax.lax.axis_size('tensor'), 1...  12.6 us
  transfers between devices with their start and end apart: 5, of which 3 were waited for; matrix products, arithmetic and copies ran while one was open for 13% of the time, Pallas kernels for 0%

profile of v1, /device:TPU:0, one launch (start us, length us, event | category | flops | bytes accessed | tf_op | source)
XLA Modules:
  0.0 582.5 jit_solution(16932664185258380720)
XLA Ops:
  8.5 2.9 collective-permute-start.1
  28.3 3.6 all-to-all-start
  33.1 12.6 %all-to-all-done = bf16[2,64,4096]{2,1,0:T(8,128)(2,1)S(1)} async-done(((bf16[2,64,4096]{2,1,0:T(8,128)(2,1)}), bf16[2,64,4096]{2,1,0:T(8,128)(2,1)S(1)}, u32[]{:S(2)}, u32[]{:S(2)}) %all-to-all-start) | async-done | bytes 1048608 | tf_op jit(solution)/shard_map/all_to_all | solution.py:61
  45.7 3.3 reshape.359
  49.0 4.0 copy.83
  53.0 3.8 fusion.13
  61.0 10.5 %fusion.1 = f32[4,16,64,128]{3,2,1,0:T(8,128)} fusion(f32[4,128,128]{2,1,0:T(8,128)S(1)} %fusion.61, f32[4,16,128]{2,1,0:T(8,128)} %bitcast.195, pred[128,128]{1,0:T(8,128)(4,1)S(1)} %fusion.54, f32[128,4,16,64]{0,3,2,1:T(8,128)S(1)} %bitcast.175, f32[128,4,16]{0,2,1:T(8,128)} %bitcast.187), kind=kOutput, calls=%fused_computation.11 | convolution fusion | flops 810024960 | bytes 4538368 | tf_op jit(solution)/shard_map/ghkij,kjghp->kighp/dot_general | solution.py:147
  74.7 36.0 %all-reduce = f32[16]{0:T(128)} all-reduce(f32[16]{0:T(128)} %dynamic-update-slice), channel_id=2, replica_groups=mesh['context'=16,'tensor'=2] {'context'}, use_global_device_ids=true, to_apply=%add | all-reduce | flops 16 | bytes 128
  110.7 19.4 %all-gather = f32[64,16,1,1]{1,3,2,0:T(1,128)} all-gather(f32[4,16,1,1]{1,3,2,0:T(1,128)} %bitcast.203), channel_id=3, replica_groups=mesh['context'=16,'tensor'=2] {'context'}, dimensions={0}, use_global_device_ids=true | all-gather | bytes 4352 | tf_op jit(solution)/shard_map/all_gather | solution.py:35
  130.2 3.2 reshape.371
  133.4 4.9 copy.96
  138.3 4.3 multiply_reduce_fusion
  144.7 4.4 fusion.3
  149.1 49.8 %all-gather.7.cloned.1.call-done = f32[16,4,16,128,64]{3,4,2,1,0:T(8,128)} async-done(((f32[1,4,16,128,64]{3,4,2,1,0:T(8,128)}), f32[16,4,16,128,64]{3,4,2,1,0:T(8,128)}) %all-gather.7.cloned.1.call-update) | async-done | bytes 33554448 | tf_op jit(solution)/shard_map/all_gather | solution.py:35
  202.2 6.8 %fusion.37 = f32[1,128,4,128]{1,3,2,0:T(8,128)} fusion(f32[1,128,4,128]{1,3,2,0:T(8,128)} %convolution_bitcast_fusion, f32[4,16,128,64]{3,2,1,0:T(8,128)} %get-tuple-element.217, bf16[128,4,16,64]{0,3,2,1:T(8,128)(2,1)S(1)} %copy-done.2, f32[4,16,128]{2,1,0:T(8,128)S(1)} %copy-done.8), kind=kOutput, calls=%fused_computation.54 | convolution fusion | flops 806420480 | bytes 3702784 | tf_op jit(solution)/shard_map/kighp,kghnp,ghki->kign/dot_general | solution.py:143
  210.8 6.9 %fusion.10 = f32[128,4,16]{0,2,1:T(8,128)} fusion(f32[1,128,4,16,64]{1,4,3,2,0:T(8,128)S(1)} %copy-done.3, f32[4,16,64,128]{3,2,1,0:T(8,128)} %fusion.1, f32[4,16,128,64]{3,2,1,0:T(8,128)} %get-tuple-element.217, f32[128,4,16]{0,2,1:T(8,128)S(1)} %bitcast.193, bf16[128,4,128,1]{2,1,0,3:T(4,128)(2,1)S(1)} %bitcast.183), kind=kOutput, calls=%fused_computation.20 | convolution fusion | flops 807395328 | bytes 6488064 | tf_op jit(solution)/shard_map/kign,kghnp,ghki->kighp/dot_general | solution.py:139
  217.8 151.2 %all-gather.5.cloned.1.call-done = f32[16,4,16,128,64]{3,4,2,1,0:T(8,128)} async-done(((f32[1,4,16,128,64]{3,4,2,1,0:T(8,128)}), f32[16,4,16,128,64]{3,4,2,1,0:T(8,128)}) %all-gather.5.cloned.1.call-update) | async-done | bytes 33554448 | tf_op jit(solution)/shard_map/all_gather | solution.py:35
  371.6 167.7 %while.40 = (s32[]{:T(128)}, f32[4,16,128,64]{3,2,1,0:T(8,128)}, s32[]{:T(128)}, f32[16,4,16]{2,1,0:T(4,128)}, f32[16,4,16,128,64]{3,4,2,1,0:T(8,128)}, /*index=5*/s32[]{:T(128)}, s32[]{:T(128)}, s32[]{:T(128)}, s32[]{:T(128)}) while((s32[]{:T(128)}, f32[4,16,128,64]{3,2,1,0:T(8,128)}, s32[]{:T(128)}, f32[16,4,16]{2,1,0:T(4,128)}, ...), condition=%wide.region_2.3_spmd, body=%wide.region_1.2_spmd.sunk | while | flops 1048582 | bytes 14680979 | solution.py:44
  373.3 2.8 copy.138
  376.7 6.0 %bitcast_add_fusion.10 = f32[4,16,128,64]{3,2,1,0:T(8,128)} fusion(f32[1,4,16,128,64]{4,3,2,1,0:T(8,128)} %copy.138, f32[4,16,128,64]{3,2,1,0:T(8,128)} %get-tuple-element.428, f32[4,16]{1,0:T(4,128)S(1)} %dynamic-slice_bitcast_fusion.4), kind=kLoop, calls=%fused_computation.clone.1 | loop fusion | flops 1048576 | bytes 6291712 | tf_op jit(solution)/shard_map/while/body/add | solution.py:50
  384.5 2.8 copy.138
  387.9 6.0 %bitcast_add_fusion.10 = f32[4,16,128,64]{3,2,1,0:T(8,128)} fusion(f32[1,4,16,128,64]{4,3,2,1,0:T(8,128)} %copy.138, f32[4,16,128,64]{3,2,1,0:T(8,128)} %get-tuple-element.428, f32[4,16]{1,0:T(4,128)S(1)} %dynamic-slice_bitcast_fusion.4), kind=kLoop, calls=%fused_computation.clone.1 | loop fusion | flops 1048576 | bytes 6291712 | tf_op jit(solution)/shard_map/while/body/add | solution.py:50
  395.7 2.8 copy.138
  399.1 6.0 %bitcast_add_fusion.10 = f32[4,16,128,64]{3,2,1,0:T(8,128)} fusion(f32[1,4,16,128,64]{4,3,2,1,0:T(8,128)} %copy.138, f32[4,16,128,64]{3,2,1,0:T(8,128)} %get-tuple-element.428, f32[4,16]{1,0:T(4,128)S(1)} %dynamic-slice_bitcast_fusion.4), kind=kLoop, calls=%fused_computation.clone.1 | loop fusion | flops 1048576 | bytes 6291712 | tf_op jit(solution)/shard_map/while/body/add | solution.py:50
  406.8 2.8 copy.138
  410.3 6.0 %bitcast_add_fusion.10 = f32[4,16,128,64]{3,2,1,0:T(8,128)} fusion(f32[1,4,16,128,64]{4,3,2,1,0:T(8,128)} %copy.138, f32[4,16,128,64]{3,2,1,0:T(8,128)} %get-tuple-element.428, f32[4,16]{1,0:T(4,128)S(1)} %dynamic-slice_bitcast_fusion.4), kind=kLoop, calls=%fused_computation.clone.1 | loop fusion | flops 1048576 | bytes 6291712 | tf_op jit(solution)/shard_map/while/body/add | solution.py:50
  418.0 2.8 copy.138
  421.5 6.0 %bitcast_add_fusion.10 = f32[4,16,128,64]{3,2,1,0:T(8,128)} fusion(f32[1,4,16,128,64]{4,3,2,1,0:T(8,128)} %copy.138, f32[4,16,128,64]{3,2,1,0:T(8,128)} %get-tuple-element.428, f32[4,16]{1,0:T(4,128)S(1)} %dynamic-slice_bitcast_fusion.4), kind=kLoop, calls=%fused_computation.clone.1 | loop fusion | flops 1048576 | bytes 6291712 | tf_op jit(solution)/shard_map/while/body/add | solution.py:50
  429.2 2.8 copy.138
  432.6 6.0 %bitcast_add_fusion.10 = f32[4,16,128,64]{3,2,1,0:T(8,128)} fusion(f32[1,4,16,128,64]{4,3,2,1,0:T(8,128)} %copy.138, f32[4,16,128,64]{3,2,1,0:T(8,128)} %get-tuple-element.428, f32[4,16]{1,0:T(4,128)S(1)} %dynamic-slice_bitcast_fusion.4), kind=kLoop, calls=%fused_computation.clone.1 | loop fusion | flops 1048576 | bytes 6291712 | tf_op jit(solution)/shard_map/while/body/add | solution.py:50
  440.4 2.8 copy.138
  443.8 6.0 %bitcast_add_fusion.10 = f32[4,16,128,64]{3,2,1,0:T(8,128)} fusion(f32[1,4,16,128,64]{4,3,2,1,0:T(8,128)} %copy.138, f32[4,16,128,64]{3,2,1,0:T(8,128)} %get-tuple-element.428, f32[4,16]{1,0:T(4,128)S(1)} %dynamic-slice_bitcast_fusion.4), kind=kLoop, calls=%fused_computation.clone.1 | loop fusion | flops 1048576 | bytes 6291712 | tf_op jit(solution)/shard_map/while/body/add | solution.py:50
  451.6 2.8 copy.138
  455.0 6.0 %bitcast_add_fusion.10 = f32[4,16,128,64]{3,2,1,0:T(8,128)} fusion(f32[1,4,16,128,64]{4,3,2,1,0:T(8,128)} %copy.138, f32[4,16,128,64]{3,2,1,0:T(8,128)} %get-tuple-element.428, f32[4,16]{1,0:T(4,128)S(1)} %dynamic-slice_bitcast_fusion.4), kind=kLoop, calls=%fused_computation.clone.1 | loop fusion | flops 1048576 | bytes 6291712 | tf_op jit(solution)/shard_map/while/body/add | solution.py:50
  462.7 2.8 copy.138
  466.2 6.0 %bitcast_add_fusion.10 = f32[4,16,128,64]{3,2,1,0:T(8,128)} fusion(f32[1,4,16,128,64]{4,3,2,1,0:T(8,128)} %copy.138, f32[4,16,128,64]{3,2,1,0:T(8,128)} %get-tuple-element.428, f32[4,16]{1,0:T(4,128)S(1)} %dynamic-slice_bitcast_fusion.4), kind=kLoop, calls=%fused_computation.clone.1 | loop fusion | flops 1048576 | bytes 6291712 | tf_op jit(solution)/shard_map/while/body/add | solution.py:50
  473.9 2.8 copy.138
  477.4 6.0 %bitcast_add_fusion.10 = f32[4,16,128,64]{3,2,1,0:T(8,128)} fusion(f32[1,4,16,128,64]{4,3,2,1,0:T(8,128)} %copy.138, f32[4,16,128,64]{3,2,1,0:T(8,128)} %get-tuple-element.428, f32[4,16]{1,0:T(4,128)S(1)} %dynamic-slice_bitcast_fusion.4), kind=kLoop, calls=%fused_computation.clone.1 | loop fusion | flops 1048576 | bytes 6291712 | tf_op jit(solution)/shard_map/while/body/add | solution.py:50
  488.5 6.0 %bitcast_add_fusion.10 = f32[4,16,128,64]{3,2,1,0:T(8,128)} fusion(f32[1,4,16,128,64]{4,3,2,1,0:T(8,128)} %copy.138, f32[4,16,128,64]{3,2,1,0:T(8,128)} %get-tuple-element.428, f32[4,16]{1,0:T(4,128)S(1)} %dynamic-slice_bitcast_fusion.4), kind=kLoop, calls=%fused_computation.clone.1 | loop fusion | flops 1048576 | bytes 6291712 | tf_op jit(solution)/shard_map/while/body/add | solution.py:50
  499.7 6.0 %bitcast_add_fusion.10 = f32[4,16,128,64]{3,2,1,0:T(8,128)} fusion(f32[1,4,16,128,64]{4,3,2,1,0:T(8,128)} %copy.138, f32[4,16,128,64]{3,2,1,0:T(8,128)} %get-tuple-element.428, f32[4,16]{1,0:T(4,128)S(1)} %dynamic-slice_bitcast_fusion.4), kind=kLoop, calls=%fused_computation.clone.1 | loop fusion | flops 1048576 | bytes 6291712 | tf_op jit(solution)/shard_map/while/body/add | solution.py:50
  507.4 2.8 copy.138
  510.9 6.0 %bitcast_add_fusion.10 = f32[4,16,128,64]{3,2,1,0:T(8,128)} fusion(f32[1,4,16,128,64]{4,3,2,1,0:T(8,128)} %copy.138, f32[4,16,128,64]{3,2,1,0:T(8,128)} %get-tuple-element.428, f32[4,16]{1,0:T(4,128)S(1)} %dynamic-slice_bitcast_fusion.4), kind=kLoop, calls=%fused_computation.clone.1 | loop fusion | flops 1048576 | bytes 6291712 | tf_op jit(solution)/shard_map/while/body/add | solution.py:50
  518.6 2.8 copy.138
  522.1 6.0 %bitcast_add_fusion.10 = f32[4,16,128,64]{3,2,1,0:T(8,128)} fusion(f32[1,4,16,128,64]{4,3,2,1,0:T(8,128)} %copy.138, f32[4,16,128,64]{3,2,1,0:T(8,128)} %get-tuple-element.428, f32[4,16]{1,0:T(4,128)S(1)} %dynamic-slice_bitcast_fusion.4), kind=kLoop, calls=%fused_computation.clone.1 | loop fusion | flops 1048576 | bytes 6291712 | tf_op jit(solution)/shard_map/while/body/add | solution.py:50
  533.2 6.0 %bitcast_add_fusion.10 = f32[4,16,128,64]{3,2,1,0:T(8,128)} fusion(f32[1,4,16,128,64]{4,3,2,1,0:T(8,128)} %copy.138, f32[4,16,128,64]{3,2,1,0:T(8,128)} %get-tuple-element.428, f32[4,16]{1,0:T(4,128)S(1)} %dynamic-slice_bitcast_fusion.4), kind=kLoop, calls=%fused_computation.clone.1 | loop fusion | flops 1048576 | bytes 6291712 | tf_op jit(solution)/shard_map/while/body/add | solution.py:50
  539.3 7.7 %multiply_reduce_fusion.1 = (f32[128,4,16]{0,2,1:T(8,128)S(1)}, f32[128,4,16]{0,2,1:T(8,128)}, bf16[1,128,4,16,64]{1,4,3,2,0:T(8,128)(2,1)S(1)}) fusion(f32[1,128,4,16,64]{1,4,3,2,0:T(8,128)} %bitcast.177, f32[128,4,16]{0,2,1:T(8,128)} %bitcast.189, f32[4,16,128,64]{3,2,1,0:T(8,128)} %get-tuple-element.216, bf16[128,4,128,1]{2,1,0,3:T(4,128)(2,1)S(1)} %bitcast.181, ...), kind=kOutput, calls=%fused_computation.30 | convolution fusion | flops 810008576 | bytes 7602176 | tf_op jit(solution)/shard_map/kjgn,kghnp,ghkj->kjghp/dot_general | solution.py:140
  547.1 17.0 %all-gather.1 = f32[16,1,64]{2,1,0:T(1,128)S(1)} all-gather(f32[1,1,64]{2,1,0:T(1,128)S(1)} %reshape.378), channel_id=1, replica_groups=mesh['context'=16,'tensor'=2] {'context'}, dimensions={0}, use_global_device_ids=true | all-gather | bytes 4352 | tf_op jit(solution)/shard_map/all_gather | solution.py:35
  564.9 6.7 %fusion.33 = f32[1,128,4,128]{1,3,2,0:T(8,128)} fusion(f32[1,128,4,128]{1,3,2,0:T(8,128)S(1)} %copy-done.5, f32[4,16,128,64]{3,2,1,0:T(8,128)} %get-tuple-element.216, f32[128,4,16,64]{0,3,2,1:T(8,128)S(1)} %bitcast.178, f32[4,16,128]{2,1,0:T(8,128)} %get-tuple-element.315, f32[128,4,16]{0,2,1:T(8,128)} %bitcast.190), kind=kOutput, calls=%fused_computation.52 | convolution fusion | flops 806420480 | bytes 4784128 | tf_op jit(solution)/shard_map/kjghp,kghnp,ghkj->kjgn/dot_general | solution.py:144
  (144 shorter events, 83.3 us)
Async XLA Ops:
  7.2 191.8 %all-gather.7.cloned.1.call-start = ((), (), s32[]{:S(2)}) async-start(), calls=%async_computation.2 | async-start | bytes 35651584 | tf_op jit(solution)/shard_map/all_gather | solution.py:35
  8.5 11.0 %collective-permute-start.1 = (s32[1]{0:T(128)}, s32[1]{0:T(128)}, u32[]{:S(2)}, u32[]{:S(2)}) collective-permute-start(s32[1]{0:T(128)} %get-tuple-element.321), channel_id=1, source_target_pairs={{0,2},{2,4},{4,6},{6,8},{8,10},{10,12},{12,14},{14,16},{16,18},{18... | collective-permute-start | bytes 20 | tf_op jit(solution)/shard_map/ppermute | solution.py:22
  11.3 10.0 %collective-permute-start = (s32[1]{0:T(128)}, s32[1]{0:T(128)}, u32[]{:S(2)}, u32[]{:S(2)}) collective-permute-start(s32[1]{0:T(128)} %get-tuple-element.320), channel_id=1, source_target_pairs={{2,0},{4,2},{6,4},{8,6},{10,8},{12,10},{14,12},{16,14},{18,16},{20... | collective-permute-start | bytes 20 | tf_op jit(solution)/shard_map/ppermute | solution.py:24
  16.5 6.1 %copy-start.9 = (f32[4,16,1,128]{3,1,2,0:T(8,128)}, f32[4,16,1,128]{3,1,2,0:T(8,128)S(1)}, u32[]{:S(2)}) copy-start(f32[4,16,1,128]{3,1,2,0:T(8,128)S(1)} %reduce_window_sum.11) | copy-start | bytes 98308
  19.3 2.7 copy-start.17
  19.3 4.1 copy-start.6
  19.5 118.8 %copy-start = (f32[128,4096]{0,1:T(8,128)}, f32[128,4096]{0,1:T(8,128)S(1)}, u32[]{:S(2)}) copy-start(f32[128,4096]{0,1:T(8,128)S(1)} %convert_element_type.47) | copy-start | bytes 6291460
  22.7 3.3 copy-start.15
  22.7 3.3 copy-start.19
  23.4 29.6 %copy-start.7 = (f32[4,16,128]{2,1,0:T(8,128)}, f32[4,16,128]{2,1,0:T(8,128)S(1)}, u32[]{:S(2)}) copy-start(f32[4,16,128]{2,1,0:T(8,128)S(1)} %get-tuple-element.316) | copy-start | bytes 98308
  28.3 17.4 %all-to-all-start = ((bf16[2,64,4096]{2,1,0:T(8,128)(2,1)}), bf16[2,64,4096]{2,1,0:T(8,128)(2,1)S(1)}, u32[]{:S(2)}, u32[]{:S(2)}) async-start(bf16[2,64,4096]{2,1,0:T(8,128)(2,1)} %pad_maximum_fusion), calls=%async_computation | async-start | bytes 2097152 | tf_op jit(solution)/shard_map/all_to_all | solution.py:61
  31.9 337.1 %all-gather.5.cloned.1.call-start = ((), (), s32[]{:S(2)}) async-start(), calls=%async_computation.1 | async-start | bytes 35651584 | tf_op jit(solution)/shard_map/all_gather | solution.py:35
  56.8 1.6 copy-start.23
  61.0 10.5 %copy-start.11 = (f32[4,128,128]{2,1,0:T(8,128)}, f32[4,128,128]{2,1,0:T(8,128)S(1)}, u32[]{:S(2)}) copy-start(f32[4,128,128]{2,1,0:T(8,128)S(1)} %fusion.61) | copy-start | bytes 786436
  133.4 4.9 copy-start.2
  138.2 4.4 copy-start.4
  138.2 6.5 %copy-start.10 = (f32[4,16,1,128]{3,1,2,0:T(8,128)S(1)}, f32[4,16,1,128]{3,1,2,0:T(8,128)}, u32[]{:S(2)}) copy-start(f32[4,16,1,128]{3,1,2,0:T(8,128)} %copy-done.9) | copy-start | bytes 98308
  138.3 6.5 %copy-start.12 = (f32[4,128,128]{2,1,0:T(8,128)S(1)}, f32[4,128,128]{2,1,0:T(8,128)}, u32[]{:S(2)}) copy-start(f32[4,128,128]{2,1,0:T(8,128)} %copy-done.11) | copy-start | bytes 786436
  201.4 0.8 copy-start.8
  202.2 8.7 %copy-start.3 = (f32[1,128,4,16,64]{1,4,3,2,0:T(8,128)S(1)}, f32[1,128,4,16,64]{1,4,3,2,0:T(8,128)}, u32[]{:S(2)}) copy-start(f32[1,128,4,16,64]{1,4,3,2,0:T(8,128)} %copy.96) | copy-start | bytes 6291460
  539.2 7.7 %copy-start.13 = (f32[128,4,16]{0,2,1:T(8,128)S(1)}, f32[128,4,16]{0,2,1:T(8,128)}, u32[]{:S(2)}) copy-start(f32[128,4,16]{0,2,1:T(8,128)} %fusion.10) | copy-start | bytes 98308
  539.2 7.7 %copy-start.16 = (f32[128]{0:T(128)S(1)}, f32[128]{0:T(128)}, u32[]{:S(2)}) copy-start(f32[128]{0:T(128)} %copy-done.15) | copy-start | bytes 1540
  539.3 24.9 %copy-start.21 = (f32[16]{0:T(128)S(1)}, f32[16]{0:T(128)}, u32[]{:S(2)}) copy-start(f32[16]{0:T(128)} %all-reduce) | copy-start | bytes 196
  539.3 25.6 %copy-start.1 = (f32[128,4096]{0,1:T(8,128)S(1)}, f32[128,4096]{0,1:T(8,128)}, u32[]{:S(2)}) copy-start(f32[128,4096]{0,1:T(8,128)} %copy-done) | copy-start | bytes 6291460
  539.3 25.6 %copy-start.5 = (f32[1,128,4,128]{1,3,2,0:T(8,128)S(1)}, f32[1,128,4,128]{1,3,2,0:T(8,128)}, u32[]{:S(2)}) copy-start(f32[1,128,4,128]{1,3,2,0:T(8,128)} %convolution_bitcast_fusion.1) | copy-start | bytes 786436
  571.6 3.1 copy-start.14
  571.6 3.1 copy-start.18
  571.6 3.1 copy-start.20
  571.6 3.1 copy-start.22
Sparse Core Ops, SparseCore 0:
  26.1 172.7 all-gather.6
  200.5 168.4 all-gather.4
